TPU v7x, 32 devices: a whole 2x2x4 slice. The times are simulated.
32 devices in a mesh: gx: 4 (over y, x), gy: 8 (over z, core).
Axes of the slice: x: 2, y: 2, z: 4, core: 2. Of those that a mesh axis runs over, the one named last changes fastest.
Arguments:
- grad_out: bfloat16 [16, 16, 64, 256], P('gx', 'gy'), may hold values from -6 to 6
- relu_mask: int32 [16, 16, 64, 256], P('gx', 'gy'), may hold values 0 or 1
- activations: bfloat16 [16, 16, 64, 256], P('gx', 'gy'), may hold values from -6 to 6
- weight: bfloat16 [27, 256, 256], P(None, 'gx'), may hold values from -0.078125 to 0.078125
Outputs:
- grad_input: bfloat16 [16, 16, 64, 256], P('gx', 'gy')
- weight_grad: float32 [27, 256, 256], P(None, 'gx', 'gy')
All inputs are finite; a program needn't handle non-finite values. No bound on the sum of `relu_mask` on one device may be relied on, other than what follows from the above.
Results may differ from a plain program's by a relative error of at most 0.001.
Values may be sent and summed in bfloat16 or wider, within the bound.
A program may use at most 64 MiB of HBM per device.

v0:
```python
import math
import jax
import jax.numpy as jnp
from jax import lax
from jax.sharding import PartitionSpec as P


def padded(shard, sides, width):
    for axis, dim in sides:
        devices, length = (lax.axis_size(axis), shard.shape[dim])
        up = [(i, (i + 1) % devices) for i in range(devices - 1)]
        down = [(j, i) for i, j in up]
        last = lax.slice_in_dim(shard, length - width, length, axis=dim)
        leading = lax.slice_in_dim(shard, 0, width, axis=dim)
        before = lax.ppermute(last, axis, up)
        after = lax.ppermute(leading, axis, down)
        shard = jnp.concatenate([before, shard, after], axis=dim)
    return shard


def tap_list():
    return [(a, b, c) for a in (-1, 0, 1) for b in (-1, 0, 1) for c in (-1, 0, 1)]


def body(grad_out, relu_mask, activations, weight):
    size_x, size_y, size_z = (grad_out.shape[0], grad_out.shape[1], grad_out.shape[2])
    out_chan = grad_out.shape[3]
    in_chan = activations.shape[3]
    cells = size_x * size_y * size_z
    gated = jnp.where(relu_mask != 0, grad_out, jnp.zeros_like(grad_out))
    grad_cycle = padded(gated, (("gx", 0), ("gy", 1)), 1)
    grad_pad = jnp.pad(grad_cycle, ((0, 0), (0, 0), (1, 1), (0, 0)))
    input_cycle = padded(activations, (("gx", 0), ("gy", 1)), 1)
    input_pad = jnp.pad(input_cycle, ((0, 0), (0, 0), (1, 1), (0, 0)))
    piece = lax.all_gather(weight, "gx", axis=1, tiled=True)
    accum = jnp.zeros((cells, piece.shape[1]), jnp.float32)
    for tap, (project_a, project_b, project_c) in enumerate(tap_list()):
        window = grad_pad[
            1 - project_a : 1 - project_a + size_x,
            1 - project_b : 1 - project_b + size_y,
            1 - project_c : 1 - project_c + size_z,
            :,
        ].reshape(cells, out_chan)
        accum = accum + lax.dot_general(
            window, piece[tap], (((1,), (1,)), ((), ())), preferred_element_type=jnp.float32
        )
    grad_input = accum.reshape(size_x, size_y, size_z, piece.shape[1]).astype(jnp.bfloat16)
    gated_flat = gated.reshape(cells, out_chan)
    terms = []
    for a, b, c in tap_list():
        shifted = input_pad[
            1 + a : 1 + a + size_x, 1 + b : 1 + b + size_y, 1 + c : 1 + c + size_z, :
        ].reshape(cells, in_chan)
        terms.append(
            lax.dot_general(
                shifted, gated_flat, (((0,), (0,)), ((), ())), preferred_element_type=jnp.float32
            )
        )
    partial_value = jnp.stack(terms, axis=0)[None]
    pieces = lax.all_to_all(partial_value, "gy", split_axis=3, concat_axis=0, tiled=True)
    section = jnp.sum(pieces, axis=0)
    summed = lax.psum_scatter(section, "gx", scatter_dimension=1, tiled=True)
    whole_cells = cells * lax.axis_size("gx") * lax.axis_size("gy")
    weight_grad = summed * (1.0 / math.sqrt(whole_cells))
    return (grad_input, weight_grad)


def solution(mesh):
    in_specs = (
        P("gx", "gy", None, None),
        P("gx", "gy", None, None),
        P("gx", "gy", None, None),
        P(None, "gx", None),
    )
    out_specs = (P("gx", "gy", None, None), P(None, "gx", "gy"))
    return jax.shard_map(body, mesh=mesh, in_specs=in_specs, out_specs=out_specs, check_vma=False)
```

profile of v0, /device:TPU:0, one launch (start us, length us, event | category | flops | bytes accessed | tf_op | source)
XLA Modules:
  0.0 302.3 jit_solution(12069150072496918049)
XLA Ops:
  8.0 4.9 %collective-permute-start.4 = (bf16[1,2,64,256]{3,2,1,0:T(8,128)(2,1)S(1)}, bf16[1,2,64,256]{3,2,1,0:T(8,128)(2,1)S(1)}, u32[]{:S(2)}, u32[]{:S(2)}) collective-permute-start(bf16[1,2,64,256]{3,2,1,0:T(8,128)(2,1)S(1)} %get-tuple-element.33), channel_id=1, source_target_pairs={{0,8},{8,16},{16,24},{1,9},{9,17},{17,25},{2,10},{10,18},{18,26},{... | collective-permute-start | bytes 196616 | tf_op jit(solution)/shard_map/ppermute | solution.py:15
  12.9 1.3 collective-permute-start.5
  15.8 3.3 %collective-permute-done.5 = bf16[1,2,64,256]{3,2,1,0:T(8,128)(2,1)S(1)} collective-permute-done((bf16[1,2,64,256]{3,2,1,0:T(8,128)(2,1)S(1)}, bf16[1,2,64,256]{3,2,1,0:T(8,128)(2,1)S(1)}, u32[]{:S(2)}, u32[]{:S(2)}) %collective-permute-start.5) | collective-permute-done | bytes 65568 | tf_op jit(solution)/shard_map/ppermute | solution.py:16
  19.1 1.3 collective-permute-start.6
  20.4 1.4 collective-permute-start.7
  21.9 1.2 compare_select_fusion
  23.1 2.6 collective-permute-done.7
  29.1 1.0 fusion.28
  32.0 1.0 fusion.26
  34.0 1.0 fusion.25
  35.0 1.0 fusion.24
  36.0 1.0 fusion.8
  42.8 1.0 fusion.18
  43.8 1.0 fusion.17
  44.8 1.0 fusion.6
  45.8 1.0 fusion.16
  46.8 1.0 fusion.15
  47.8 1.0 fusion.5
  49.7 1.0 fusion.13
  52.7 16.9 %copy.13 = f32[1,27,256,256]{2,0,1,3:T(1,128)} copy(f32[1,27,256,256]{3,2,1,0:T(8,128)} %bitcast.136) | data formatting | bytes 14155776 | tf_op jit(solution)/shard_map/broadcast_in_dim | solution.py:59
  69.5 7.6 %all-to-all-start = ((f32[1,27,256,256]{2,0,1,3:T(1,128)}), f32[1,27,256,256]{2,0,1,3:T(1,128)}, u32[]{:S(2)}, u32[]{:S(2)}) async-start(f32[1,27,256,256]{2,0,1,3:T(1,128)} %copy.13), calls=%async_computation | async-start | bytes 14155776 | tf_op jit(solution)/shard_map/all_to_all | solution.py:60
  78.0 4.3 %collective-permute-start = (bf16[1,2,64,256]{3,2,1,0:T(8,128)(2,1)S(1)}, bf16[1,2,64,256]{3,2,1,0:T(8,128)(2,1)S(1)}, u32[]{:S(2)}, u32[]{:S(2)}) collective-permute-start(bf16[1,2,64,256]{3,2,1,0:T(8,128)(2,1)S(1)} %get-tuple-element.36), channel_id=1, source_target_pairs={{0,8},{8,16},{16,24},{1,9},{9,17},{17,25},{2,10},{10,18},{18,26},{... | collective-permute-start | bytes 196616 | tf_op jit(solution)/shard_map/ppermute | solution.py:15
  82.3 1.3 collective-permute-start.1
  84.4 4.7 %collective-permute-done.1 = bf16[1,2,64,256]{3,2,1,0:T(8,128)(2,1)S(1)} collective-permute-done((bf16[1,2,64,256]{3,2,1,0:T(8,128)(2,1)S(1)}, bf16[1,2,64,256]{3,2,1,0:T(8,128)(2,1)S(1)}, u32[]{:S(2)}, u32[]{:S(2)}) %collective-permute-start.1) | collective-permute-done | bytes 65568 | tf_op jit(solution)/shard_map/ppermute | solution.py:16
  89.2 2.2 collective-permute-start.2
  91.4 1.5 collective-permute-start.3
  92.9 2.8 collective-permute-done.3
  96.3 1.0 fusion.72
  97.3 1.9 fusion.71
  99.1 29.2 %all-gather.2.cloned.1.call-done = bf16[27,256,256]{2,1,0:T(8,128)(2,1)} async-done(((bf16[27,64,256]{2,1,0:T(8,128)(2,1)}), bf16[27,256,256]{2,1,0:T(8,128)(2,1)}) %all-gather.2.cloned.1.call-update) | async-done | bytes 3538960 | tf_op jit(solution)/shard_map/all_gather | solution.py:35
  128.4 1.3 fusion.62
  129.7 1.2 fusion.61
  130.9 1.3 convolution_add_fusion.23
  132.2 1.3 convolution_add_fusion.22
  138.0 95.4 %all-to-all-done = f32[1,27,256,256]{2,0,1,3:T(1,128)} async-done(((f32[1,27,256,256]{2,0,1,3:T(1,128)}), f32[1,27,256,256]{2,0,1,3:T(1,128)}, u32[]{:S(2)}, u32[]{:S(2)}) %all-to-all-start) | async-done | bytes 7077920 | tf_op jit(solution)/shard_map/all_to_all | solution.py:60
  233.4 6.8 %copy.14 = f32[1,27,256,256]{2,3,1,0:T(8,128)} copy(f32[1,27,256,256]{2,0,1,3:T(1,128)} %all-to-all-done) | data formatting | bytes 14155776 | tf_op jit(solution)/shard_map/all_to_all | solution.py:60
  240.2 3.9 %reduce_sum.9 = f32[27,256,32]{1,2,0:T(8,128)S(1)} reduce(f32[27,256,8,32]{1,3,2,0:T(8,128)} %bitcast.385, f32[]{:T(128)} %constant.2.clone.1), dimensions={2}, to_apply=%region_0.1 | reduce | flops 1548288 | bytes 7962628 | tf_op jit(solution)/shard_map/reduce_sum | solution.py:61
  244.1 4.4 %copy.43 = f32[27,256,32]{2,0,1:T(8,128)} copy(f32[27,256,32]{1,2,0:T(8,128)S(1)} %reduce_sum.9) | data formatting | bytes 1769472
  248.5 4.2 %reshape.170 = f32[256,864]{1,0:T(8,128)} reshape(f32[256,27,32]{2,1,0:T(8,128)} %bitcast.386) | data formatting | bytes 1769472
  252.7 1.2 fusion.60
  253.9 1.2 convolution_add_fusion.5
  255.0 1.2 convolution_add_fusion.4
  256.2 1.2 fusion.1
  257.4 1.2 convolution_add_fusion.2
  258.6 1.2 convolution_add_fusion.1
  259.7 1.9 fusion.3
  261.6 31.3 %reduce-scatter.4.cloned.1.call-done = f32[64,864]{1,0:T(8,128)} async-done(((f32[256,864]{1,0:T(8,128)}), f32[64,864]{1,0:T(8,128)}) %reduce-scatter.4.cloned.1.call-update) | async-done | bytes 221200
  292.9 1.3 reshape.171
  (81 shorter events, 25.3 us)
Async XLA Ops:
  8.0 6.8 %collective-permute-start.4 = (bf16[1,2,64,256]{3,2,1,0:T(8,128)(2,1)S(1)}, bf16[1,2,64,256]{3,2,1,0:T(8,128)(2,1)S(1)}, u32[]{:S(2)}, u32[]{:S(2)}) collective-permute-start(bf16[1,2,64,256]{3,2,1,0:T(8,128)(2,1)S(1)} %get-tuple-element.33), channel_id=1, source_target_pairs={{0,8},{8,16},{16,24},{1,9},{9,17},{17,25},{2,10},{10,18},{18,26},{... | collective-permute-start | bytes 196616 | tf_op jit(solution)/shard_map/ppermute | solution.py:15
  12.9 6.2 %collective-permute-start.5 = (bf16[1,2,64,256]{3,2,1,0:T(8,128)(2,1)S(1)}, bf16[1,2,64,256]{3,2,1,0:T(8,128)(2,1)S(1)}, u32[]{:S(2)}, u32[]{:S(2)}) collective-permute-start(bf16[1,2,64,256]{3,2,1,0:T(8,128)(2,1)S(1)} %get-tuple-element.32), channel_id=1, source_target_pairs={{8,0},{16,8},{24,16},{9,1},{17,9},{25,17},{10,2},{18,10},{26,18},{... | collective-permute-start | bytes 196616 | tf_op jit(solution)/shard_map/ppermute | solution.py:16
  19.1 3.9 %collective-permute-start.6 = (bf16[6,1,64,256]{3,2,1,0:T(8,128)(2,1)S(1)}, bf16[6,1,64,256]{3,2,1,0:T(8,128)(2,1)S(1)}, u32[]{:S(2)}, u32[]{:S(2)}) collective-permute-start(bf16[6,1,64,256]{3,2,1,0:T(8,128)(2,1)S(1)} %get-tuple-element.26), channel_id=1, source_target_pairs={{0,1},{1,2},{2,3},{3,4},{4,5},{5,6},{6,7},{8,9},{9,10},{10,11},{11... | collective-permute-start | bytes 589832 | tf_op jit(solution)/shard_map/ppermute | solution.py:15
  20.4 9.6 %copy-start.1 = (bf16[4,2,64,256]{3,2,1,0:T(8,128)(2,1)S(1)}, bf16[4,2,64,256]{3,2,1,0:T(8,128)(2,1)}, u32[]{:S(2)}) copy-start(bf16[4,2,64,256]{3,2,1,0:T(8,128)(2,1)} %param.6) | copy-start | bytes 786436
  20.4 5.3 %collective-permute-start.7 = (bf16[6,1,64,256]{3,2,1,0:T(8,128)(2,1)S(1)}, bf16[6,1,64,256]{3,2,1,0:T(8,128)(2,1)S(1)}, u32[]{:S(2)}, u32[]{:S(2)}) collective-permute-start(bf16[6,1,64,256]{3,2,1,0:T(8,128)(2,1)S(1)} %get-tuple-element.27), channel_id=1, source_target_pairs={{1,0},{2,1},{3,2},{4,3},{5,4},{6,5},{7,6},{9,8},{10,9},{11,10},{12... | collective-permute-start | bytes 589832 | tf_op jit(solution)/shard_map/ppermute | solution.py:16
  69.5 163.8 %all-to-all-start = ((f32[1,27,256,256]{2,0,1,3:T(1,128)}), f32[1,27,256,256]{2,0,1,3:T(1,128)}, u32[]{:S(2)}, u32[]{:S(2)}) async-start(f32[1,27,256,256]{2,0,1,3:T(1,128)} %copy.13), calls=%async_computation | async-start | bytes 14155776 | tf_op jit(solution)/shard_map/all_to_all | solution.py:60
  77.2 51.2 %all-gather.2.cloned.1.call-start = ((), (), s32[]{:S(2)}) async-start(), calls=%async_computation.2 | async-start | bytes 4423680 | tf_op jit(solution)/shard_map/all_gather | solution.py:35
  77.9 215.0 %reduce-scatter.4.cloned.1.call-start = ((), (), s32[]{:S(2)}) async-start(), calls=%async_computation.3 | async-start | bytes 1146880
  78.0 6.4 %collective-permute-start = (bf16[1,2,64,256]{3,2,1,0:T(8,128)(2,1)S(1)}, bf16[1,2,64,256]{3,2,1,0:T(8,128)(2,1)S(1)}, u32[]{:S(2)}, u32[]{:S(2)}) collective-permute-start(bf16[1,2,64,256]{3,2,1,0:T(8,128)(2,1)S(1)} %get-tuple-element.36), channel_id=1, source_target_pairs={{0,8},{8,16},{16,24},{1,9},{9,17},{17,25},{2,10},{10,18},{18,26},{... | collective-permute-start | bytes 196616 | tf_op jit(solution)/shard_map/ppermute | solution.py:15
  82.3 6.8 %collective-permute-start.1 = (bf16[1,2,64,256]{3,2,1,0:T(8,128)(2,1)S(1)}, bf16[1,2,64,256]{3,2,1,0:T(8,128)(2,1)S(1)}, u32[]{:S(2)}, u32[]{:S(2)}) collective-permute-start(bf16[1,2,64,256]{3,2,1,0:T(8,128)(2,1)S(1)} %get-tuple-element.37), channel_id=1, source_target_pairs={{8,0},{16,8},{24,16},{9,1},{17,9},{25,17},{10,2},{18,10},{26,18},{... | collective-permute-start | bytes 196616 | tf_op jit(solution)/shard_map/ppermute | solution.py:16
  89.2 3.7 %collective-permute-start.2 = (bf16[6,1,64,256]{3,2,1,0:T(8,128)(2,1)S(1)}, bf16[6,1,64,256]{3,2,1,0:T(8,128)(2,1)S(1)}, u32[]{:S(2)}, u32[]{:S(2)}) collective-permute-start(bf16[6,1,64,256]{3,2,1,0:T(8,128)(2,1)S(1)} %get-tuple-element.30), channel_id=1, source_target_pairs={{0,1},{1,2},{2,3},{3,4},{4,5},{5,6},{6,7},{8,9},{9,10},{10,11},{11... | collective-permute-start | bytes 589832 | tf_op jit(solution)/shard_map/ppermute | solution.py:15
  91.4 4.3 %collective-permute-start.3 = (bf16[6,1,64,256]{3,2,1,0:T(8,128)(2,1)S(1)}, bf16[6,1,64,256]{3,2,1,0:T(8,128)(2,1)S(1)}, u32[]{:S(2)}, u32[]{:S(2)}) collective-permute-start(bf16[6,1,64,256]{3,2,1,0:T(8,128)(2,1)S(1)} %get-tuple-element.31), channel_id=1, source_target_pairs={{1,0},{2,1},{3,2},{4,3},{5,4},{6,5},{7,6},{9,8},{10,9},{11,10},{12... | collective-permute-start | bytes 589832 | tf_op jit(solution)/shard_map/ppermute | solution.py:16
  128.4 5.1 %copy-start = (bf16[27,256,256]{2,1,0:T(8,128)(2,1)S(1)}, bf16[27,256,256]{2,1,0:T(8,128)(2,1)}, u32[]{:S(2)}) copy-start(bf16[27,256,256]{2,1,0:T(8,128)(2,1)} %all-gather.2.cloned.1.call-done) | copy-start | bytes 10616836
  128.4 5.1 %copy-start.13 = (bf16[4,2,64,256]{3,2,1,0:T(8,128)(2,1)S(1)}, bf16[4,2,64,256]{3,2,1,0:T(8,128)(2,1)}, u32[]{:S(2)}) copy-start(bf16[4,2,64,256]{3,2,1,0:T(8,128)(2,1)} %get-tuple-element.17) | copy-start | bytes 786436
  129.7 4.4 %copy-start.12 = (bf16[4,2,64,256]{3,2,1,0:T(8,128)(2,1)S(1)}, bf16[4,2,64,256]{3,2,1,0:T(8,128)(2,1)}, u32[]{:S(2)}) copy-start(bf16[4,2,64,256]{3,2,1,0:T(8,128)(2,1)} %get-tuple-element.15) | copy-start | bytes 786436
  130.9 3.5 %copy-start.7 = (bf16[4,2,64,256]{3,2,1,0:T(8,128)(2,1)S(1)}, bf16[4,2,64,256]{3,2,1,0:T(8,128)(2,1)}, u32[]{:S(2)}) copy-start(bf16[4,2,64,256]{3,2,1,0:T(8,128)(2,1)} %get-tuple-element.22) | copy-start | bytes 786436
  132.2 2.5 copy-start.11
  133.5 1.4 copy-start.10
  133.8 1.4 copy-start.4
  134.1 1.4 copy-start.9
  134.4 1.4 copy-start.8
  134.9 1.4 copy-start.6
  135.2 1.4 copy-start.5
  135.8 1.4 copy-start.3
  136.1 1.4 copy-start.2
Sparse Core Ops, SparseCore 0:
  79.8 48.5 all-gather.1
  252.8 39.9 reduce-scatter.3
where the time goes:
time: 304 us; the launch traced here: 302 us
  waiting for transfers between devices  171 us (56%)
  matrix products  44.5 us (15%)
  local copies, waits for them, and re-layouts  39 us (13%)
  starting transfers between devices  25.8 us (8%)
  between operations  14.6 us (5%)
  other arithmetic  7.02 us (2%)
    all_to_all x1, waiting for transfers between devices, body(): lax.all_to_all(partial_value, 'gy', split_axis=3, concat_axis=0, tiled=True)  95.4 us
    unnamed x3, waiting for transfers between devices  32 us
    all_gather x1, waiting for transfers between devices, body(): piece = lax.all_gather(weight, 'gx', axis=1, tiled=True)  29.2 us
    dot_general x27, matrix products, body(): lax.dot_general(shifted, gated_flat, (((0,), (0,)), ((), ())), preferred_...  26.5 us
    dot_general x27, matrix products, body(): lax.dot_general(window, piece[tap], (((1,), (1,)), ((), ())), preferred_e...  18.1 us
    broadcast_in_dim x1, local copies, waits for them, and re-layouts, body(): partial_value = jnp.stack(terms, axis=0)[None]  16.9 us
    ppermute x4, waiting for transfers between devices, padded(): after = lax.ppermute(leading, axis, down)  13.4 us
    ppermute x4, starting transfers between devices, padded(): before = lax.ppermute(last, axis, up)  12.7 us
  transfers between devices with their start and end apart: 11, of which 9 were waited for; matrix products, arithmetic and copies ran while one was open for 8% of the time, Pallas kernels for 0%

commit v1 on v0

--- a/solution.py
+++ b/solution.py
@@ -57,7 +57,9 @@
             )
         )
     partial_value = jnp.stack(terms, axis=0)[None]
-    pieces = lax.all_to_all(partial_value, "gy", split_axis=3, concat_axis=0, tiled=True)
+    parts = jnp.split(partial_value, lax.axis_size("gy"), axis=3)
+    got = lax.all_to_all(jnp.stack(parts), "gy", 0, 0)
+    pieces = jnp.concatenate(got, axis=0)
     section = jnp.sum(pieces, axis=0)
     summed = lax.psum_scatter(section, "gx", scatter_dimension=1, tiled=True)
     whole_cells = cells * lax.axis_size("gx") * lax.axis_size("gy")

time: 304 us -> 271 us (0.89)
  matrix products: 44.5 us -> 27.7 us
  local copies, waits for them, and re-layouts: 39 us -> 23.7 us
    dot_general x27, matrix products: 26.5 us -> 7.63 us  [body(): lax.dot_general(shifted, gated_flat, (((0,), (0,)), ((), ())), preferred_...]
    broadcast_in_dim x1 -> x0, local copies, waits for them, and re-layouts: 16.9 us -> none  [body(): partial_value = jnp.stack(terms, axis=0)[None]]
    unnamed x34 -> x39, local copies, waits for them, and re-layouts: 11.5 us -> 18.5 us
    all_to_all x1 -> x0, local copies, waits for them, and re-layouts: 6.83 us -> none  [body(): lax.all_to_all(partial_value, 'gy', split_axis=3, concat_axis=0, tiled=True)]
  transfers between devices with their start and end apart: 11 -> 11, of which waited for: 9 -> 9; matrix products, arithmetic and copies ran while one was open for 8% -> 10% of each run, Pallas kernels for 0% -> 0%
where the time goes in v1:
time: 271 us; the launch traced here: 270 us
  waiting for transfers between devices  171 us (63%)
  matrix products  27.7 us (10%)
  starting transfers between devices  25.7 us (9%)
  local copies, waits for them, and re-layouts  23.7 us (9%)
  between operations  14.6 us (5%)
  other arithmetic  6.92 us (3%)
    all_to_all x1, waiting for transfers between devices, body(): got = lax.all_to_all(jnp.stack(parts), 'gy', 0, 0)  93.4 us
    unnamed x3, waiting for transfers between devices  34.2 us
    all_gather x1, waiting for transfers between devices, body(): piece = lax.all_gather(weight, 'gx', axis=1, tiled=True)  29 us
    dot_general x27, matrix products, body(): lax.dot_general(window, piece[tap], (((1,), (1,)), ((), ())), preferred_e...  20.1 us
    unnamed x39, local copies, waits for them, and re-layouts  18.5 us
    ppermute x4, waiting for transfers between devices, padded(): after = lax.ppermute(leading, axis, down)  13.4 us
    ppermute x4, starting transfers between devices, padded(): before = lax.ppermute(last, axis, up)  12.7 us
    dot_general x27, matrix products, body(): lax.dot_general(shifted, gated_flat, (((0,), (0,)), ((), ())), preferred_...  7.63 us
  transfers between devices with their start and end apart: 11, of which 9 were waited for; matrix products, arithmetic and copies ran while one was open for 10% of the time, Pallas kernels for 0%

profile of v1, /device:TPU:0, one launch (start us, length us, event | category | flops | bytes accessed | tf_op | source)
XLA Modules:
  0.0 270.0 jit_solution(8340023863182563140)
XLA Ops:
  7.2 0.9 fusion.84
  8.1 4.9 %collective-permute-start.4 = (bf16[1,2,64,256]{3,2,1,0:T(8,128)(2,1)S(1)}, bf16[1,2,64,256]{3,2,1,0:T(8,128)(2,1)S(1)}, u32[]{:S(2)}, u32[]{:S(2)}) collective-permute-start(bf16[1,2,64,256]{3,2,1,0:T(8,128)(2,1)S(1)} %get-tuple-element.33), channel_id=1, source_target_pairs={{0,8},{8,16},{16,24},{1,9},{9,17},{17,25},{2,10},{10,18},{18,26},{... | collective-permute-start | bytes 196616 | tf_op jit(solution)/shard_map/ppermute | solution.py:15
  13.0 1.3 collective-permute-start.5
  14.9 1.0 constant_dynamic-update-slice_fusion.1
  15.8 3.3 %collective-permute-done.5 = bf16[1,2,64,256]{3,2,1,0:T(8,128)(2,1)S(1)} collective-permute-done((bf16[1,2,64,256]{3,2,1,0:T(8,128)(2,1)S(1)}, bf16[1,2,64,256]{3,2,1,0:T(8,128)(2,1)S(1)}, u32[]{:S(2)}, u32[]{:S(2)}) %collective-permute-start.5) | collective-permute-done | bytes 65568 | tf_op jit(solution)/shard_map/ppermute | solution.py:16
  19.2 1.3 collective-permute-start.6
  20.5 1.3 collective-permute-start.7
  21.8 1.2 compare_select_fusion
  23.0 2.6 collective-permute-done.7
  33.8 1.0 fusion.38
  34.8 1.0 fusion.37
  35.9 1.0 fusion.36
  36.9 1.0 fusion.35
  37.9 1.0 fusion.34
  38.9 1.0 fusion.33
  39.9 1.1 fusion.32
  40.9 1.0 fusion.31
  41.9 7.6 %all-to-all-start = ((f32[8,1,27,256,32]{3,4,2,1,0:T(8,128)}), f32[8,1,27,256,32]{3,4,2,1,0:T(8,128)}, u32[]{:S(2)}, u32[]{:S(2)}) async-start(f32[8,1,27,256,32]{3,4,2,1,0:T(8,128)} %fusion.31), calls=%async_computation | async-start | bytes 14155776 | tf_op jit(solution)/shard_map/all_to_all | solution.py:61
  50.3 4.3 %collective-permute-start = (bf16[1,2,64,256]{3,2,1,0:T(8,128)(2,1)S(1)}, bf16[1,2,64,256]{3,2,1,0:T(8,128)(2,1)S(1)}, u32[]{:S(2)}, u32[]{:S(2)}) collective-permute-start(bf16[1,2,64,256]{3,2,1,0:T(8,128)(2,1)S(1)} %get-tuple-element.36), channel_id=1, source_target_pairs={{0,8},{8,16},{16,24},{1,9},{9,17},{17,25},{2,10},{10,18},{18,26},{... | collective-permute-start | bytes 196616 | tf_op jit(solution)/shard_map/ppermute | solution.py:15
  54.6 1.3 collective-permute-start.1
  55.9 0.8 collective-permute-done
  56.8 4.7 %collective-permute-done.1 = bf16[1,2,64,256]{3,2,1,0:T(8,128)(2,1)S(1)} collective-permute-done((bf16[1,2,64,256]{3,2,1,0:T(8,128)(2,1)S(1)}, bf16[1,2,64,256]{3,2,1,0:T(8,128)(2,1)S(1)}, u32[]{:S(2)}, u32[]{:S(2)}) %collective-permute-start.1) | collective-permute-done | bytes 65568 | tf_op jit(solution)/shard_map/ppermute | solution.py:16
  61.5 2.2 collective-permute-start.2
  63.7 1.5 collective-permute-start.3
  65.3 2.8 %collective-permute-done.3 = bf16[6,1,64,256]{3,2,1,0:T(8,128)(2,1)S(1)} collective-permute-done((bf16[6,1,64,256]{3,2,1,0:T(8,128)(2,1)S(1)}, bf16[6,1,64,256]{3,2,1,0:T(8,128)(2,1)S(1)}, u32[]{:S(2)}, u32[]{:S(2)}) %collective-permute-start.3) | collective-permute-done | bytes 196640 | tf_op jit(solution)/shard_map/ppermute | solution.py:16
  68.6 1.1 fusion.80
  69.7 2.0 fusion.79
  71.8 29.0 %all-gather.2.cloned.1.call-done = bf16[27,256,256]{2,1,0:T(8,128)(2,1)} async-done(((bf16[27,64,256]{2,1,0:T(8,128)(2,1)}), bf16[27,256,256]{2,1,0:T(8,128)(2,1)}) %all-gather.2.cloned.1.call-update) | async-done | bytes 3538960 | tf_op jit(solution)/shard_map/all_gather | solution.py:35
  100.8 1.3 fusion.69
  102.1 1.3 fusion.70
  103.4 1.2 convolution_add_fusion.23
  104.7 1.3 convolution_add_fusion.22
  106.0 1.2 convolution_add_fusion.21
  107.3 1.2 fusion.2
  112.3 93.4 %all-to-all-done = f32[8,1,27,256,32]{3,4,2,1,0:T(8,128)} async-done(((f32[8,1,27,256,32]{3,4,2,1,0:T(8,128)}), f32[8,1,27,256,32]{3,4,2,1,0:T(8,128)}, u32[]{:S(2)}, u32[]{:S(2)}) %all-to-all-start) | async-done | bytes 7077920 | tf_op jit(solution)/shard_map/all_to_all | solution.py:61
  205.7 3.8 %reduce_sum.9 = f32[27,256,32]{1,2,0:T(8,128)S(1)} reduce(f32[8,1,27,256,32]{3,4,2,1,0:T(8,128)} %all-to-all-done, f32[]{:T(128)} %constant.2.clone.1), dimensions={0,1}, to_apply=%region_0.1 | reduce | flops 1548288 | bytes 7962628 | tf_op jit(solution)/shard_map/reduce_sum | solution.py:63
  209.6 4.4 %copy.33 = f32[27,256,32]{2,0,1:T(8,128)} copy(f32[27,256,32]{1,2,0:T(8,128)S(1)} %reduce_sum.9) | data formatting | bytes 1769472
  214.0 4.2 %reshape.170 = f32[256,864]{1,0:T(8,128)} reshape(f32[256,27,32]{2,1,0:T(8,128)} %bitcast.419) | data formatting | bytes 1769472
  218.1 1.2 fusion.68
  219.3 1.2 convolution_add_fusion.5
  220.5 1.2 convolution_add_fusion.4
  221.7 1.2 fusion.1
  222.8 1.2 convolution_add_fusion.2
  224.0 1.2 convolution_add_fusion.1
  225.2 1.9 fusion.3
  227.0 33.5 %reduce-scatter.4.cloned.1.call-done = f32[64,864]{1,0:T(8,128)} async-done(((f32[256,864]{1,0:T(8,128)}), f32[64,864]{1,0:T(8,128)}) %reduce-scatter.4.cloned.1.call-update) | async-done | bytes 221200
  260.5 1.3 reshape.171
  262.4 0.8 broadcast_multiply_fusion
  (85 shorter events, 14.4 us)
Async XLA Ops:
  7.2 20.1 %copy-start.12 = (bf16[4,2,64,256]{3,2,1,0:T(8,128)(2,1)S(1)}, bf16[4,2,64,256]{3,2,1,0:T(8,128)(2,1)}, u32[]{:S(2)}) copy-start(bf16[4,2,64,256]{3,2,1,0:T(8,128)(2,1)} %param.6) | copy-start | bytes 786436
  8.1 6.8 %collective-permute-start.4 = (bf16[1,2,64,256]{3,2,1,0:T(8,128)(2,1)S(1)}, bf16[1,2,64,256]{3,2,1,0:T(8,128)(2,1)S(1)}, u32[]{:S(2)}, u32[]{:S(2)}) collective-permute-start(bf16[1,2,64,256]{3,2,1,0:T(8,128)(2,1)S(1)} %get-tuple-element.33), channel_id=1, source_target_pairs={{0,8},{8,16},{16,24},{1,9},{9,17},{17,25},{2,10},{10,18},{18,26},{... | collective-permute-start | bytes 196616 | tf_op jit(solution)/shard_map/ppermute | solution.py:15
  13.0 6.2 %collective-permute-start.5 = (bf16[1,2,64,256]{3,2,1,0:T(8,128)(2,1)S(1)}, bf16[1,2,64,256]{3,2,1,0:T(8,128)(2,1)S(1)}, u32[]{:S(2)}, u32[]{:S(2)}) collective-permute-start(bf16[1,2,64,256]{3,2,1,0:T(8,128)(2,1)S(1)} %get-tuple-element.32), channel_id=1, source_target_pairs={{8,0},{16,8},{24,16},{9,1},{17,9},{25,17},{10,2},{18,10},{26,18},{... | collective-permute-start | bytes 196616 | tf_op jit(solution)/shard_map/ppermute | solution.py:16
  19.2 3.8 %collective-permute-start.6 = (bf16[6,1,64,256]{3,2,1,0:T(8,128)(2,1)S(1)}, bf16[6,1,64,256]{3,2,1,0:T(8,128)(2,1)S(1)}, u32[]{:S(2)}, u32[]{:S(2)}) collective-permute-start(bf16[6,1,64,256]{3,2,1,0:T(8,128)(2,1)S(1)} %get-tuple-element.26), channel_id=1, source_target_pairs={{0,1},{1,2},{2,3},{3,4},{4,5},{5,6},{6,7},{8,9},{9,10},{10,11},{11... | collective-permute-start | bytes 589832 | tf_op jit(solution)/shard_map/ppermute | solution.py:15
  20.5 5.1 %collective-permute-start.7 = (bf16[6,1,64,256]{3,2,1,0:T(8,128)(2,1)S(1)}, bf16[6,1,64,256]{3,2,1,0:T(8,128)(2,1)S(1)}, u32[]{:S(2)}, u32[]{:S(2)}) collective-permute-start(bf16[6,1,64,256]{3,2,1,0:T(8,128)(2,1)S(1)} %get-tuple-element.27), channel_id=1, source_target_pairs={{1,0},{2,1},{3,2},{4,3},{5,4},{6,5},{7,6},{9,8},{10,9},{11,10},{12... | collective-permute-start | bytes 589832 | tf_op jit(solution)/shard_map/ppermute | solution.py:16
  41.9 163.8 %all-to-all-start = ((f32[8,1,27,256,32]{3,4,2,1,0:T(8,128)}), f32[8,1,27,256,32]{3,4,2,1,0:T(8,128)}, u32[]{:S(2)}, u32[]{:S(2)}) async-start(f32[8,1,27,256,32]{3,4,2,1,0:T(8,128)} %fusion.31), calls=%async_computation | async-start | bytes 14155776 | tf_op jit(solution)/shard_map/all_to_all | solution.py:61
  49.5 51.2 %all-gather.2.cloned.1.call-start = ((), (), s32[]{:S(2)}) async-start(), calls=%async_computation.2 | async-start | bytes 4423680 | tf_op jit(solution)/shard_map/all_gather | solution.py:35
  50.3 210.2 %reduce-scatter.4.cloned.1.call-start = ((), (), s32[]{:S(2)}) async-start(), calls=%async_computation.3 | async-start | bytes 1146880
  50.3 6.4 %collective-permute-start = (bf16[1,2,64,256]{3,2,1,0:T(8,128)(2,1)S(1)}, bf16[1,2,64,256]{3,2,1,0:T(8,128)(2,1)S(1)}, u32[]{:S(2)}, u32[]{:S(2)}) collective-permute-start(bf16[1,2,64,256]{3,2,1,0:T(8,128)(2,1)S(1)} %get-tuple-element.36), channel_id=1, source_target_pairs={{0,8},{8,16},{16,24},{1,9},{9,17},{17,25},{2,10},{10,18},{18,26},{... | collective-permute-start | bytes 196616 | tf_op jit(solution)/shard_map/ppermute | solution.py:15
  54.6 6.8 %collective-permute-start.1 = (bf16[1,2,64,256]{3,2,1,0:T(8,128)(2,1)S(1)}, bf16[1,2,64,256]{3,2,1,0:T(8,128)(2,1)S(1)}, u32[]{:S(2)}, u32[]{:S(2)}) collective-permute-start(bf16[1,2,64,256]{3,2,1,0:T(8,128)(2,1)S(1)} %get-tuple-element.37), channel_id=1, source_target_pairs={{8,0},{16,8},{24,16},{9,1},{17,9},{25,17},{10,2},{18,10},{26,18},{... | collective-permute-start | bytes 196616 | tf_op jit(solution)/shard_map/ppermute | solution.py:16
  61.5 3.7 %collective-permute-start.2 = (bf16[6,1,64,256]{3,2,1,0:T(8,128)(2,1)S(1)}, bf16[6,1,64,256]{3,2,1,0:T(8,128)(2,1)S(1)}, u32[]{:S(2)}, u32[]{:S(2)}) collective-permute-start(bf16[6,1,64,256]{3,2,1,0:T(8,128)(2,1)S(1)} %get-tuple-element.30), channel_id=1, source_target_pairs={{0,1},{1,2},{2,3},{3,4},{4,5},{5,6},{6,7},{8,9},{9,10},{10,11},{11... | collective-permute-start | bytes 589832 | tf_op jit(solution)/shard_map/ppermute | solution.py:15
  63.7 4.4 %collective-permute-start.3 = (bf16[6,1,64,256]{3,2,1,0:T(8,128)(2,1)S(1)}, bf16[6,1,64,256]{3,2,1,0:T(8,128)(2,1)S(1)}, u32[]{:S(2)}, u32[]{:S(2)}) collective-permute-start(bf16[6,1,64,256]{3,2,1,0:T(8,128)(2,1)S(1)} %get-tuple-element.31), channel_id=1, source_target_pairs={{1,0},{2,1},{3,2},{4,3},{5,4},{6,5},{7,6},{9,8},{10,9},{11,10},{12... | collective-permute-start | bytes 589832 | tf_op jit(solution)/shard_map/ppermute | solution.py:16
  100.7 7.8 %copy-start = (bf16[27,256,256]{2,1,0:T(8,128)(2,1)S(1)}, bf16[27,256,256]{2,1,0:T(8,128)(2,1)}, u32[]{:S(2)}) copy-start(bf16[27,256,256]{2,1,0:T(8,128)(2,1)} %all-gather.2.cloned.1.call-done) | copy-start | bytes 10616836
  100.7 7.8 %copy-start.11 = (bf16[4,2,64,256]{3,2,1,0:T(8,128)(2,1)S(1)}, bf16[4,2,64,256]{3,2,1,0:T(8,128)(2,1)}, u32[]{:S(2)}) copy-start(bf16[4,2,64,256]{3,2,1,0:T(8,128)(2,1)} %get-tuple-element.15) | copy-start | bytes 786436
  100.8 8.0 %copy-start.6 = (bf16[4,2,64,256]{3,2,1,0:T(8,128)(2,1)S(1)}, bf16[4,2,64,256]{3,2,1,0:T(8,128)(2,1)}, u32[]{:S(2)}) copy-start(bf16[4,2,64,256]{3,2,1,0:T(8,128)(2,1)} %get-tuple-element.22) | copy-start | bytes 786436
  100.8 8.3 %copy-start.10 = (bf16[4,2,64,256]{3,2,1,0:T(8,128)(2,1)S(1)}, bf16[4,2,64,256]{3,2,1,0:T(8,128)(2,1)}, u32[]{:S(2)}) copy-start(bf16[4,2,64,256]{3,2,1,0:T(8,128)(2,1)} %get-tuple-element.14) | copy-start | bytes 786436
  100.8 8.6 %copy-start.9 = (bf16[4,2,64,256]{3,2,1,0:T(8,128)(2,1)S(1)}, bf16[4,2,64,256]{3,2,1,0:T(8,128)(2,1)}, u32[]{:S(2)}) copy-start(bf16[4,2,64,256]{3,2,1,0:T(8,128)(2,1)} %get-tuple-element.13) | copy-start | bytes 786436
  100.8 8.9 %copy-start.3 = (bf16[4,2,64,256]{3,2,1,0:T(8,128)(2,1)S(1)}, bf16[4,2,64,256]{3,2,1,0:T(8,128)(2,1)}, u32[]{:S(2)}) copy-start(bf16[4,2,64,256]{3,2,1,0:T(8,128)(2,1)} %get-tuple-element.39) | copy-start | bytes 786436
  102.1 7.8 %copy-start.8 = (bf16[4,2,64,256]{3,2,1,0:T(8,128)(2,1)S(1)}, bf16[4,2,64,256]{3,2,1,0:T(8,128)(2,1)}, u32[]{:S(2)}) copy-start(bf16[4,2,64,256]{3,2,1,0:T(8,128)(2,1)} %get-tuple-element.12) | copy-start | bytes 786436
  104.7 5.5 %copy-start.7 = (bf16[4,2,64,256]{3,2,1,0:T(8,128)(2,1)S(1)}, bf16[4,2,64,256]{3,2,1,0:T(8,128)(2,1)}, u32[]{:S(2)}) copy-start(bf16[4,2,64,256]{3,2,1,0:T(8,128)(2,1)} %get-tuple-element.11) | copy-start | bytes 786436
  107.2 3.5 %copy-start.5 = (bf16[4,2,64,256]{3,2,1,0:T(8,128)(2,1)S(1)}, bf16[4,2,64,256]{3,2,1,0:T(8,128)(2,1)}, u32[]{:S(2)}) copy-start(bf16[4,2,64,256]{3,2,1,0:T(8,128)(2,1)} %get-tuple-element.10) | copy-start | bytes 786436
  107.3 3.7 %copy-start.4 = (bf16[4,2,64,256]{3,2,1,0:T(8,128)(2,1)S(1)}, bf16[4,2,64,256]{3,2,1,0:T(8,128)(2,1)}, u32[]{:S(2)}) copy-start(bf16[4,2,64,256]{3,2,1,0:T(8,128)(2,1)} %get-tuple-element.9) | copy-start | bytes 786436
  108.8 2.7 %copy-start.2 = (bf16[4,2,64,256]{3,2,1,0:T(8,128)(2,1)S(1)}, bf16[4,2,64,256]{3,2,1,0:T(8,128)(2,1)}, u32[]{:S(2)}) copy-start(bf16[4,2,64,256]{3,2,1,0:T(8,128)(2,1)} %get-tuple-element.8) | copy-start | bytes 786436
  109.4 2.7 %copy-start.1 = (bf16[4,2,64,256]{3,2,1,0:T(8,128)(2,1)S(1)}, bf16[4,2,64,256]{3,2,1,0:T(8,128)(2,1)}, u32[]{:S(2)}) copy-start(bf16[4,2,64,256]{3,2,1,0:T(8,128)(2,1)} %get-tuple-element.40) | copy-start | bytes 786436
Sparse Core Ops, SparseCore 0:
  52.2 48.5 all-gather.1
  218.3 42.2 reduce-scatter.3
